TPU v7x, 128 devices: a whole 4x4x4 slice. The times are simulated.
128 devices in a mesh: row: 4 (over x), col: 32 (over y, z, core).
Axes of the slice: x: 4, y: 4, z: 4, core: 2. Of those that a mesh axis runs over, the one named last changes fastest.
Arguments:
- ancestor_inverse: float32 [16384, 16384], P('col', 'row'), as said below
- panels: float32 [2, 16384, 512], P(None, ('col', 'row')), may hold values from -0.1875 to 0.1875
- pattern: int32 [2, 128, 2], replicated, may hold values 0 or 1
- diag_inverse: float32 [2, 512, 512], replicated, may hold values from -6 to 6
- link_panel: float32 [512, 512], replicated, may hold values from -0.25 to 0.25
- block_list: int32 [32, 4, 32], P('col', 'row'), may hold values from 0 to 7
- gauge_owner: int32 [32, 4, 32], P('col', 'row'), may hold values from 0 to 31, each once within a row
- gauge_weight: float32 [4, 32, 512], P('row', 'col'), may hold values from -0.25 to 0.25
Outputs:
- y_first: float32 [16384, 512], P(('col', 'row'))
- diag_first: float32 [512, 512], replicated
- y_second: float32 [16384, 512], P(('col', 'row'))
- cross_second: float32 [512, 512], replicated
- diag_second: float32 [512, 512], replicated
- gauge_response: float32 [4, 32, 512], P('row', 'col')
Inputs may be any that keep to these rules, and one draw needn't show every extreme that they name: `ancestor_inverse`: with its columns put in natural order the matrix is symmetric.
All inputs are finite; a program needn't handle non-finite values.
Results may differ from a plain program's by a relative error of at most 0.000092.
Values sent between devices are 32-bit elements; how exact they have to be, the bound alone decides.
No kernel may reach another device: no remote copies, remote signals or barrier semaphores. Data moves between devices by JAX's collectives and lax.ppermute only.
A program may use at most 128 MiB of HBM per device.

v0:
```python
import jax
import jax.numpy as jnp
from jax import lax
from jax.sharding import PartitionSpec as P

NIB = 8
HIGHEST_PRECISION = lax.Precision.HIGHEST


def matmul(left, right):
    return jnp.dot(left, right, precision=HIGHEST_PRECISION, preferred_element_type=jnp.float32)


def inner_product(left, right):
    return lax.dot_general(
        left,
        right,
        (((0,), (0,)), ((), ())),
        precision=HIGHEST_PRECISION,
        preferred_element_type=jnp.float32,
    )


def apply_pattern(panel, pattern_step, seg_index):
    tile_flags = lax.dynamic_index_in_dim(pattern_step, seg_index, 0, keepdims=False).astype(
        jnp.float32
    )
    seg_rows, panel_width = panel.shape
    tile_count = tile_flags.shape[0]
    shaped = (
        panel.reshape(seg_rows, tile_count, panel_width // tile_count) * tile_flags[None, :, None]
    )
    return shaped.reshape(seg_rows, panel_width)


def inverse_slab(ancestor, panel_seg):
    partial_rows = matmul(ancestor, lax.all_gather(panel_seg, "col", axis=0, tiled=True))
    return lax.psum_scatter(partial_rows, "row", scatter_dimension=0, tiled=True)


def local(
    ancestor_inverse,
    panels,
    pattern,
    diag_inverse,
    link_panel,
    block_list,
    gauge_owner,
    gauge_weight,
):
    grid_rows = lax.axis_size("row")
    grid_cols = lax.axis_size("col")
    seg_index = lax.axis_index("col") * grid_rows + lax.axis_index("row")
    first_panel = apply_pattern(panels[0], pattern[0], seg_index)
    second_panel = apply_pattern(panels[1], pattern[1], seg_index)
    y_first = -inverse_slab(ancestor_inverse, first_panel)
    first_terms = lax.psum(inner_product(first_panel, y_first), ("row", "col"))
    diag_first = diag_inverse[0] - first_terms
    cross_terms = lax.psum(inner_product(y_first, second_panel), ("row", "col"))
    y_second = -(inverse_slab(ancestor_inverse, second_panel) + matmul(y_first, link_panel))
    second_terms = lax.psum(inner_product(second_panel, y_second), ("row", "col"))
    cross_second = -(cross_terms + matmul(diag_first, link_panel))
    diag_second = diag_inverse[1] - second_terms - inner_product(link_panel, cross_second)
    seg_rows, panel_width = y_second.shape
    block_rows = seg_rows // NIB
    blocks = y_second.reshape(NIB, block_rows * panel_width)
    owners = gauge_owner[0, 0]
    picks = block_list[0, 0]
    owner_match = (owners[None, :] == jnp.arange(grid_cols, dtype=jnp.int32)[:, None]).astype(
        jnp.float32
    )
    block_match = (picks[:, None] == jnp.arange(NIB, dtype=jnp.int32)[None, :]).astype(jnp.float32)
    selector = matmul(owner_match, block_match)
    outgoing = matmul(selector, blocks)
    received = lax.all_to_all(outgoing, "col", split_axis=0, concat_axis=0, tiled=True)
    received_rows = received.reshape(grid_cols * block_rows, panel_width)
    weights = gauge_weight[0, 0]
    gauge_response = matmul(weights[None, :], received_rows).reshape(1, 1, panel_width)
    return (y_first, diag_first, y_second, cross_second, diag_second, gauge_response)


def solution(mesh):
    in_specs = (
        P("col", "row"),
        P(None, ("col", "row"), None),
        P(),
        P(),
        P(),
        P("col", "row", None),
        P("col", "row", None),
        P("row", "col", None),
    )
    out_specs = (
        P(("col", "row"), None),
        P(),
        P(("col", "row"), None),
        P(),
        P(),
        P("row", "col", None),
    )
    return jax.shard_map(local, mesh=mesh, in_specs=in_specs, out_specs=out_specs, check_vma=False)
```

profile of v0, /device:TPU:1, one launch (start us, length us, event | category | flops | bytes accessed | tf_op | source)
XLA Modules:
  0.0 363.5 jit_solution(13496992720899328515)
XLA Ops:
  7.2 0.8 fusion.12
  8.4 1.9 bitcast_multiply_fusion
  10.3 0.7 all-gather.5.cloned.1.call-update
  11.1 56.5 %all-gather.3.cloned.1.call-done = f32[4096,512]{1,0:T(8,128)} async-done(((f32[128,512]{1,0:T(8,128)}), f32[4096,512]{1,0:T(8,128)}) %all-gather.3.cloned.1.call-update) | async-done | bytes 8388624 | tf_op jit(solution)/shard_map/all_gather | solution.py:37
  67.5 30.1 %convolution_bitcast_fusion.3 = f32[512,512]{0,1:T(8,128)} fusion(f32[4096,512]{1,0:T(8,128)} %all-gather.3.cloned.1.call-done, f32[512,4096]{1,0:T(8,128)} %param.8), kind=kOutput, calls=%fused_computation.6 | convolution fusion | flops 12884901888 | bytes 17825792 | tf_op jit(solution)/shard_map/dot_general | solution.py:11
  97.9 25.0 %all-gather.5.cloned.1.call-done = f32[4096,512]{1,0:T(8,128)} async-done(((f32[128,512]{1,0:T(8,128)}), f32[4096,512]{1,0:T(8,128)}) %all-gather.5.cloned.1.call-update) | async-done | bytes 8388624 | tf_op jit(solution)/shard_map/all_gather | solution.py:37
  122.9 30.1 %convolution_bitcast_fusion.2 = f32[512,512]{0,1:T(8,128)} fusion(f32[4096,512]{1,0:T(8,128)} %all-gather.5.cloned.1.call-done, f32[512,4096]{1,0:T(8,128)} %param.8), kind=kOutput, calls=%fused_computation.5 | convolution fusion | flops 12884901888 | bytes 17825792 | tf_op jit(solution)/shard_map/dot_general | solution.py:11
  153.0 0.3 all-reduce.3.cloned.1.call-start
  153.3 21.1 %reduce-scatter.5.cloned.1.call-done = f32[128,512]{0,1:T(8,128)} async-done(((f32[512,512]{0,1:T(8,128)}), f32[128,512]{0,1:T(8,128)}) %reduce-scatter.5.cloned.1.call-update) | async-done | bytes 262160 | tf_op jit(solution)/shard_map/reduce_scatter | solution.py:38
  174.4 2.8 fusion.2
  177.3 2.0 fusion.13
  179.3 2.9 fusion.7
  182.2 3.0 fusion.10
  185.6 1.0 convolution_bitcast_fusion
  186.7 2.1 copy.26
  188.7 9.0 %all-to-all-start = ((f32[32,1,8192]{2,1,0:T(1,128)}), f32[32,1,8192]{2,1,0:T(1,128)S(1)}, u32[]{:S(2)}, u32[]{:S(2)}) async-start(f32[32,1,8192]{2,1,0:T(1,128)} %copy.26), calls=%async_computation.2 | async-start | bytes 2097152 | tf_op jit(solution)/shard_map/all_to_all | solution.py:75
  197.8 0.8 copy.27
  198.6 17.2 %all-to-all-done = f32[32,1,8192]{2,1,0:T(1,128)S(1)} async-done(((f32[32,1,8192]{2,1,0:T(1,128)}), f32[32,1,8192]{2,1,0:T(1,128)S(1)}, u32[]{:S(2)}, u32[]{:S(2)}) %all-to-all-start) | async-done | bytes 1048608 | tf_op jit(solution)/shard_map/all_to_all | solution.py:75
  215.9 2.6 reduce.2
  218.7 1.2 convolution_bitcast_fusion.4
  219.9 127.0 %all-reduce.3.cloned.1.call-done = (f32[512,512]{1,0:T(8,128)}, f32[512,512]{1,0:T(8,128)}, f32[512,512]{1,0:T(8,128)}) async-done(((f32[512,512]{1,0:T(8,128)}, f32[512,512]{1,0:T(8,128)}, f32[512,512]{1,0:T(8,128)}), (f32[512,512]{1,0:T(8,128)}, f32[512,512]{1,0:T(8,128)}, f32[512,512]{1,0:T(8,128)})) %all-reduce.3.cloned.1.call-update) | async-done | bytes 3145744 | tf_op jit(solution)/shard_map/psum | solution.py:57
  346.9 1.7 bitcast_subtract_fusion.1
  348.6 3.5 fusion.1
  352.2 4.8 %fusion = f32[512,512]{1,0:T(8,128)} fusion(f32[512,512]{1,0:T(8,128)S(1)} %fusion.1, f32[512,512]{1,0:T(8,128)S(1)} %copy-done, f32[512,512]{1,0:T(8,128)} %get-tuple-element.26, f32[2,512,512]{2,1,0:T(8,128)} %param.11), kind=kOutput, calls=%fused_computation.2 | convolution fusion | flops 1611137024 | bytes 5242880 | tf_op jit(solution)/shard_map/dot_general | solution.py:15
  (39 shorter events, 1.5 us)
Async XLA Ops:
  7.2 167.3 %copy-start = (f32[512,512]{1,0:T(8,128)S(1)}, f32[512,512]{1,0:T(8,128)}, u32[]{:S(2)}) copy-start(f32[512,512]{1,0:T(8,128)} %param.12) | copy-start | bytes 3145732
  7.2 60.4 %all-gather.3.cloned.1.call-start = ((), (), s32[]{:S(2)}) async-start(), calls=%async_computation.3 | async-start | bytes 8650752 | tf_op jit(solution)/shard_map/all_gather | solution.py:37
  10.3 112.6 %all-gather.5.cloned.1.call-start = ((), (), s32[]{:S(2)}) async-start(), calls=%async_computation.5 | async-start | bytes 8650752 | tf_op jit(solution)/shard_map/all_gather | solution.py:37
  11.0 142.3 %reduce-scatter.3.cloned.1.call-start = ((), (), s32[]{:S(2)}) async-start(), calls=%async_computation.4 | async-start | bytes 1310720 | tf_op jit(solution)/shard_map/reduce_scatter | solution.py:38
  97.6 79.6 %copy-start.4 = (f32[128,512]{1,0:T(8,128)S(1)}, f32[128,512]{1,0:T(8,128)}, u32[]{:S(2)}) copy-start(f32[128,512]{1,0:T(8,128)} %get-tuple-element.27) | copy-start | bytes 786436
  97.6 84.5 %copy-start.5 = (f32[128,512]{1,0:T(8,128)S(1)}, f32[128,512]{1,0:T(8,128)}, u32[]{:S(2)}) copy-start(f32[128,512]{1,0:T(8,128)} %get-tuple-element.28) | copy-start | bytes 786436
  97.7 76.8 %reduce-scatter.5.cloned.1.call-start = ((), (), s32[]{:S(2)}) async-start(), calls=%async_computation.6 | async-start | bytes 1310720 | tf_op jit(solution)/shard_map/reduce_scatter | solution.py:38
  153.0 32.2 %copy-start.8 = (s32[1,1,32]{2,1,0:T(1,128)S(1)}, s32[1,1,32]{2,1,0:T(1,128)}, u32[]{:S(2)}) copy-start(s32[1,1,32]{2,1,0:T(1,128)} %param.13) | copy-start | bytes 388
  153.0 32.2 %copy-start.9 = (s32[1,1,32]{2,1,0:T(1,128)S(1)}, s32[1,1,32]{2,1,0:T(1,128)}, u32[]{:S(2)}) copy-start(s32[1,1,32]{2,1,0:T(1,128)} %param.14) | copy-start | bytes 388
  153.0 193.8 %all-reduce.3.cloned.1.call-start = ((), (), s32[]{:S(2)}) async-start(), calls=%async_computation.7 | async-start | bytes 6291456 | tf_op jit(solution)/shard_map/psum | solution.py:57
  153.3 44.4 %copy-start.3 = (f32[128,512]{0,1:T(8,128)S(1)}, f32[128,512]{0,1:T(8,128)}, u32[]{:S(2)}) copy-start(f32[128,512]{0,1:T(8,128)} %reduce-scatter.3.cloned.1.call-done) | copy-start | bytes 786436
  182.2 36.5 %copy-start.7 = (f32[1,1,512]{2,1,0:T(1,128)S(1)}, f32[1,1,512]{2,1,0:T(1,128)}, u32[]{:S(2)}) copy-start(f32[1,1,512]{2,1,0:T(1,128)} %param.15) | copy-start | bytes 6148
  185.6 3.2 copy-start.6
  188.7 27.2 %all-to-all-start = ((f32[32,1,8192]{2,1,0:T(1,128)}), f32[32,1,8192]{2,1,0:T(1,128)S(1)}, u32[]{:S(2)}, u32[]{:S(2)}) async-start(f32[32,1,8192]{2,1,0:T(1,128)} %copy.26), calls=%async_computation.2 | async-start | bytes 2097152 | tf_op jit(solution)/shard_map/all_to_all | solution.py:75
  348.6 8.3 %copy-start.1 = (f32[512,512]{1,0:T(8,128)}, f32[512,512]{1,0:T(8,128)S(1)}, u32[]{:S(2)}) copy-start(f32[512,512]{1,0:T(8,128)S(1)} %bitcast_subtract_fusion.1) | copy-start | bytes 3145732
  352.2 4.8 %copy-start.2 = (f32[512,512]{1,0:T(8,128)}, f32[512,512]{1,0:T(8,128)S(1)}, u32[]{:S(2)}) copy-start(f32[512,512]{1,0:T(8,128)S(1)} %fusion.1) | copy-start | bytes 3145732
Sparse Core Ops, SparseCore 0:
  10.9 56.6 all-gather.2
  70.4 52.5 all-gather.4
  125.9 21.1 reduce-scatter.2
  153.2 21.2 reduce-scatter.4
  185.3 161.5 all-reduce.2
where the time goes:
time: 364 us; the launch traced here: 363 us
  waiting for transfers between devices  248 us (68%)
  matrix products  81.6 us (22%)
  between operations  14 us (4%)
  starting transfers between devices  9.63 us (3%)
  other arithmetic  6.45 us (2%)
  local copies, waits for them, and re-layouts  4.26 us (1%)
    psum x1, waiting for transfers between devices, local(): first_terms = lax.psum(inner_product(first_panel, y_first), ('row', 'col'))  127 us
    all_gather x2, waiting for transfers between devices, inverse_slab(): lax.all_gather(panel_seg, 'col', axis=0, tiled=True)  81.5 us
    dot_general x7, matrix products, matmul(): jnp.dot(left, right, precision=HIGHEST_PRECISION, preferred_element_type=...  69 us
    reduce_scatter x2, waiting for transfers between devices, inverse_slab(): lax.psum_scatter(partial_rows, 'row', scatter_dimension=0, tiled=True)  21.1 us
    all_to_all x1, waiting for transfers between devices, local(): lax.all_to_all(outgoing, 'col', split_axis=0, concat_axis=0, tiled=True)  17.2 us
    dot_general x4, matrix products, inner_product(): lax.dot_general(left, right, (((0,), (0,)), ((), ())), precision=HIGHEST_...  12.6 us
    all_to_all x1, starting transfers between devices, local(): lax.all_to_all(outgoing, 'col', split_axis=0, concat_axis=0, tiled=True)  9.03 us
  transfers between devices with their start and end apart: 6, of which 5 were waited for; matrix products, arithmetic and copies ran while one was open for 19% of the time, Pallas kernels for 0%

commit v1 on v0

--- a/solution.py
+++ b/solution.py
@@ -34,7 +34,12 @@
 
 
 def inverse_slab(ancestor, panel_seg):
-    partial_rows = matmul(ancestor, lax.all_gather(panel_seg, "col", axis=0, tiled=True))
+    partial_rows = matmul(
+        ancestor,
+        jnp.concatenate(
+            lax.all_to_all(jnp.stack([panel_seg] * lax.axis_size("col")), "col", 0, 0), axis=0
+        ),
+    )
     return lax.psum_scatter(partial_rows, "row", scatter_dimension=0, tiled=True)
 
 

time: 364 us -> 491 us (1.35)
  blocking collectives: 0 us -> 105 us
  waiting for transfers between devices: 248 us -> 260 us
  local copies, waits for them, and re-layouts: 4.26 us -> 9.64 us
    all_to_all x0 -> x1, blocking collectives: none -> 105 us  [inverse_slab(): lax.all_to_all(jnp.stack([panel_seg] * lax.axis_size('col')), 'col', 0, 0)]
    all_gather x2 -> x0, waiting for transfers between devices: 81.5 us -> none  [inverse_slab(): lax.all_gather(panel_seg, 'col', axis=0, tiled=True)]
    all_to_all x0 -> x1, waiting for transfers between devices: none -> 76.3 us  [inverse_slab(): lax.all_to_all(jnp.stack([panel_seg] * lax.axis_size('col')), 'col', 0, 0)]
    reduce_scatter x2, waiting for transfers between devices: 21.1 us -> 39.1 us  [inverse_slab(): lax.psum_scatter(partial_rows, 'row', scatter_dimension=0, tiled=True)]
    another operation x0 -> x2, local copies, waits for them, and re-layouts: none -> 5.37 us  [inverse_slab(): jnp.stack([panel_seg] * lax.axis_size('col'))]
  transfers between devices with their start and end apart: 6 -> 5, of which waited for: 5 -> 4; matrix products, arithmetic and copies ran while one was open for 19% -> 14% of each run, Pallas kernels for 0% -> 0%
where the time goes in v1:
time: 491 us; the launch traced here: 490 us
  waiting for transfers between devices  260 us (53%)
  blocking collectives  105 us (21%)
  matrix products  81.7 us (17%)
  starting transfers between devices  14.4 us (3%)
  between operations  13.9 us (3%)
  local copies, waits for them, and re-layouts  9.64 us (2%)
  other arithmetic  5.65 us (1%)
    psum x1, waiting for transfers between devices, local(): first_terms = lax.psum(inner_product(first_panel, y_first), ('row', 'col'))  127 us
    all_to_all x1, blocking collectives, inverse_slab(): lax.all_to_all(jnp.stack([panel_seg] * lax.axis_size('col')), 'col', 0, 0)  105 us
    all_to_all x1, waiting for transfers between devices, inverse_slab(): lax.all_to_all(jnp.stack([panel_seg] * lax.axis_size('col')), 'col', 0, 0)  76.3 us
    dot_general x7, matrix products, matmul(): jnp.dot(left, right, precision=HIGHEST_PRECISION, preferred_element_type=...  69 us
    reduce_scatter x2, waiting for transfers between devices, inverse_slab(): lax.psum_scatter(partial_rows, 'row', scatter_dimension=0, tiled=True)  39.1 us
    all_to_all x1, waiting for transfers between devices, local(): lax.all_to_all(outgoing, 'col', split_axis=0, concat_axis=0, tiled=True)  17.3 us
    dot_general x4, matrix products, inner_product(): lax.dot_general(left, right, (((0,), (0,)), ((), ())), precision=HIGHEST_...  12.7 us
  transfers between devices with their start and end apart: 5, of which 4 were waited for; matrix products, arithmetic and copies ran while one was open for 14% of the time, Pallas kernels for 0%

profile of v1, /device:TPU:1, one launch (start us, length us, event | category | flops | bytes accessed | tf_op | source)
XLA Modules:
  0.0 490.0 jit_solution(15511132333516795812)
XLA Ops:
  8.3 1.1 multiply_bitcast_fusion
  9.4 1.1 stack.6
  10.5 105.1 %all_to_all.19 = f32[32,128,512]{2,1,0:T(8,128)} all-to-all(f32[32,128,512]{2,1,0:T(8,128)S(1)} %stack.6), channel_id=1, replica_groups=mesh['row'=4,'col'=32] {'col'}, dimensions={0} | all-to-all | bytes 16777216 | tf_op jit(solution)/shard_map/all_to_all | solution.py:40
  115.6 4.3 stack.7
  119.9 4.8 all-to-all-start.1
  124.7 30.1 %convolution_bitcast_fusion.3 = f32[512,512]{0,1:T(8,128)} fusion(f32[4096,512]{1,0:T(8,128)} %bitcast.59, f32[512,4096]{1,0:T(8,128)} %param.8), kind=kOutput, calls=%fused_computation.6 | convolution fusion | flops 12884901888 | bytes 17825792 | tf_op jit(solution)/shard_map/dot_general | solution.py:11
  155.0 76.3 %all-to-all-done.1 = f32[32,128,512]{2,1,0:T(8,128)} async-done(((f32[32,128,512]{2,1,0:T(8,128)}), f32[32,128,512]{2,1,0:T(8,128)}, u32[]{:S(2)}, u32[]{:S(2)}) %all-to-all-start.1) | async-done | bytes 8388640 | tf_op jit(solution)/shard_map/all_to_all | solution.py:40
  231.4 30.1 %convolution_bitcast_fusion.2 = f32[512,512]{0,1:T(8,128)} fusion(f32[4096,512]{1,0:T(8,128)} %bitcast.6, f32[512,4096]{1,0:T(8,128)} %param.8), kind=kOutput, calls=%fused_computation.5 | convolution fusion | flops 12884901888 | bytes 17825792 | tf_op jit(solution)/shard_map/dot_general | solution.py:11
  261.8 39.1 %reduce-scatter.5.cloned.1.call-done = f32[128,512]{0,1:T(8,128)} async-done(((f32[512,512]{0,1:T(8,128)}), f32[128,512]{0,1:T(8,128)}) %reduce-scatter.5.cloned.1.call-update) | async-done | bytes 262160 | tf_op jit(solution)/shard_map/reduce_scatter | solution.py:43
  300.9 2.8 fusion.2
  303.7 2.0 fusion.4
  305.8 2.9 fusion.5
  308.7 3.0 fusion.3
  312.1 1.0 convolution_bitcast_fusion
  313.2 2.1 copy.26
  315.2 9.1 %all-to-all-start.2 = ((f32[32,1,8192]{2,1,0:T(1,128)}), f32[32,1,8192]{2,1,0:T(1,128)S(1)}, u32[]{:S(2)}, u32[]{:S(2)}) async-start(f32[32,1,8192]{2,1,0:T(1,128)} %copy.26), calls=%async_computation.4 | async-start | bytes 2097152 | tf_op jit(solution)/shard_map/all_to_all | solution.py:80
  324.4 0.8 copy.27
  325.2 17.3 %all-to-all-done.2 = f32[32,1,8192]{2,1,0:T(1,128)S(1)} async-done(((f32[32,1,8192]{2,1,0:T(1,128)}), f32[32,1,8192]{2,1,0:T(1,128)S(1)}, u32[]{:S(2)}, u32[]{:S(2)}) %all-to-all-start.2) | async-done | bytes 1048608 | tf_op jit(solution)/shard_map/all_to_all | solution.py:80
  342.5 2.6 reduce.2
  345.2 1.2 convolution_bitcast_fusion.4
  346.5 126.9 %all-reduce.3.cloned.1.call-done = (f32[512,512]{1,0:T(8,128)}, f32[512,512]{1,0:T(8,128)}, f32[512,512]{1,0:T(8,128)}) async-done(((f32[512,512]{1,0:T(8,128)}, f32[512,512]{1,0:T(8,128)}, f32[512,512]{1,0:T(8,128)}), (f32[512,512]{1,0:T(8,128)}, f32[512,512]{1,0:T(8,128)}, f32[512,512]{1,0:T(8,128)})) %all-reduce.3.cloned.1.call-update) | async-done | bytes 3145744 | tf_op jit(solution)/shard_map/psum | solution.py:62
  473.4 1.7 bitcast_subtract_fusion.1
  475.2 3.5 fusion.1
  478.7 4.8 fusion
  (36 shorter events, 2.4 us)
Async XLA Ops:
  7.2 293.7 %copy-start = (f32[512,512]{1,0:T(8,128)S(1)}, f32[512,512]{1,0:T(8,128)}, u32[]{:S(2)}) copy-start(f32[512,512]{1,0:T(8,128)} %param.12) | copy-start | bytes 3145732
  119.9 111.5 %all-to-all-start.1 = ((f32[32,128,512]{2,1,0:T(8,128)}), f32[32,128,512]{2,1,0:T(8,128)}, u32[]{:S(2)}, u32[]{:S(2)}) async-start(f32[32,128,512]{2,1,0:T(8,128)} %stack.7), calls=%async_computation.2 | async-start | bytes 16777216 | tf_op jit(solution)/shard_map/all_to_all | solution.py:40
  124.6 137.1 %reduce-scatter.3.cloned.1.call-start = ((), (), s32[]{:S(2)}) async-start(), calls=%async_computation.5 | async-start | bytes 1310720 | tf_op jit(solution)/shard_map/reduce_scatter | solution.py:43
  154.8 146.1 %reduce-scatter.5.cloned.1.call-start = ((), (), s32[]{:S(2)}) async-start(), calls=%async_computation.6 | async-start | bytes 1310720 | tf_op jit(solution)/shard_map/reduce_scatter | solution.py:43
  231.4 72.4 %copy-start.4 = (f32[2,128,512]{2,1,0:T(8,128)S(1)}, f32[2,128,512]{2,1,0:T(8,128)}, u32[]{:S(2)}) copy-start(f32[2,128,512]{2,1,0:T(8,128)} %param.9) | copy-start | bytes 1572868
  261.5 50.2 %copy-start.7 = (s32[1,1,32]{2,1,0:T(1,128)S(1)}, s32[1,1,32]{2,1,0:T(1,128)}, u32[]{:S(2)}) copy-start(s32[1,1,32]{2,1,0:T(1,128)} %param.13) | copy-start | bytes 388
  261.5 50.2 %copy-start.8 = (s32[1,1,32]{2,1,0:T(1,128)S(1)}, s32[1,1,32]{2,1,0:T(1,128)}, u32[]{:S(2)}) copy-start(s32[1,1,32]{2,1,0:T(1,128)} %param.14) | copy-start | bytes 388
  261.5 211.9 %all-reduce.3.cloned.1.call-start = ((), (), s32[]{:S(2)}) async-start(), calls=%async_computation.7 | async-start | bytes 6291456 | tf_op jit(solution)/shard_map/psum | solution.py:62
  261.8 62.5 %copy-start.3 = (f32[128,512]{0,1:T(8,128)S(1)}, f32[128,512]{0,1:T(8,128)}, u32[]{:S(2)}) copy-start(f32[128,512]{0,1:T(8,128)} %reduce-scatter.3.cloned.1.call-done) | copy-start | bytes 786436
  308.7 36.6 %copy-start.6 = (f32[1,1,512]{2,1,0:T(1,128)S(1)}, f32[1,1,512]{2,1,0:T(1,128)}, u32[]{:S(2)}) copy-start(f32[1,1,512]{2,1,0:T(1,128)} %param.15) | copy-start | bytes 6148
  312.1 3.2 copy-start.5
  315.2 27.2 %all-to-all-start.2 = ((f32[32,1,8192]{2,1,0:T(1,128)}), f32[32,1,8192]{2,1,0:T(1,128)S(1)}, u32[]{:S(2)}, u32[]{:S(2)}) async-start(f32[32,1,8192]{2,1,0:T(1,128)} %copy.26), calls=%async_computation.4 | async-start | bytes 2097152 | tf_op jit(solution)/shard_map/all_to_all | solution.py:80
  475.2 8.3 %copy-start.1 = (f32[512,512]{1,0:T(8,128)}, f32[512,512]{1,0:T(8,128)S(1)}, u32[]{:S(2)}) copy-start(f32[512,512]{1,0:T(8,128)S(1)} %bitcast_subtract_fusion.1) | copy-start | bytes 3145732
  478.7 4.8 copy-start.2
Sparse Core Ops, SparseCore 0:
  154.9 23.2 reduce-scatter.2
  261.6 39.2 reduce-scatter.4
  311.8 161.6 all-reduce.2
